TPU v7x, 512 devices: a whole 4x8x8 slice. The times are simulated.
512 devices in a mesh: chan: 32 (over z, y_hi), seg: 16 (over x, y_lo, core).
Axes of the slice: x: 4, y: 8 (y_hi: 4, y_lo: 2; y = y_hi * 2 + y_lo), z: 8, core: 2. Of those that a mesh axis runs over, the one named last changes fastest.
Arguments:
- strain: float32 [1024, 40000], P('chan', 'seg')
- source_channels: int32 [32], replicated, may hold values from 0 to 1023, as said below
Outputs:
- stack: float32 [32, 1024, 501], P('seg', 'chan')
Inputs may be any that keep to these rules, and one draw needn't show every extreme that they name: `source_channels`: distinct channels; channel 0 and channel 1024 - 1 are always among them.
All inputs are finite; a program needn't handle non-finite values.
Results may differ from a plain program's by a relative error of at most 0.0001.
Values sent between devices are 32-bit elements; how exact they have to be, the bound alone decides.
A program may use at most 64 MiB of HBM per device.

v0:
```python
import math
import jax
import jax.numpy as jnp
from jax import lax
from jax.sharding import PartitionSpec as P

SEG_LEN = 625
TAPS = 63
MAXLAG = 250
cutoff = 0.1
water_level = 0.5
epsilon = 1e-06
block_width = 128


def from_behind(value, axis, steps):
    count = lax.axis_size(axis)
    leading, last = (max(0, -steps), min(count, count - steps))
    return lax.ppermute(value, axis, [(source, source + steps) for source in range(leading, last)])


def tap_shape(position, count):
    window = 0.54 - 0.46 * jnp.cos(2.0 * math.pi * position / (count - 1))
    return window * 2.0 * cutoff * jnp.sinc(2.0 * cutoff * (position - (count - 1) / 2.0))


def band_table(count):
    total = jnp.sum(tap_shape(jnp.arange(count).astype(jnp.float32), count))
    span = 5 * block_width
    offsets = jnp.arange(span)[:, None] - 4 * jnp.arange(block_width)[None, :]
    valid = (offsets >= 0) & (offsets <= count - 1)
    values = tap_shape((count - 1 - offsets).astype(jnp.float32), count) / total
    return jnp.where(valid, values, 0.0)


def decimate(extended, seg_len):
    channel_count = extended.shape[0]
    blocks = -(-seg_len // block_width)
    span = 5 * block_width
    stride = 4 * block_width
    needed = stride * (blocks - 1) + span
    extended = jnp.pad(extended, ((0, 0), (0, needed - extended.shape[1])))
    windows = jnp.stack(
        [
            extended[:, stride * block_index : stride * block_index + span]
            for block_index in range(blocks)
        ],
        axis=1,
    )
    outputs = jnp.einsum("rbi,im->rbm", windows, band_table(TAPS), precision=lax.Precision.HIGHEST)
    return outputs.reshape(channel_count, blocks * block_width)[:, :seg_len]


def forward_table(seg_len, block_index):
    samples = jnp.arange(seg_len)[:, None]
    freqs = block_index * block_width + jnp.arange(block_width)[None, :]
    phase = jnp.mod(samples * freqs, 2 * seg_len).astype(jnp.float32) * (math.pi / seg_len)
    valid = freqs <= seg_len
    return jnp.concatenate(
        [jnp.where(valid, jnp.cos(phase), 0.0), jnp.where(valid, -jnp.sin(phase), 0.0)], axis=1
    )


def inverse_table(block_index, factor):
    freqs = block_index * block_width + jnp.arange(block_width)[:, None]
    lag_values = jnp.arange(2 * MAXLAG + 1)[None, :] - MAXLAG
    phase = jnp.mod(freqs * lag_values, 2 * SEG_LEN).astype(jnp.float32) * (math.pi / SEG_LEN)
    weight = jnp.where((freqs == 0) | (freqs == SEG_LEN), 1.0, 2.0) * factor
    weight = jnp.where(freqs <= SEG_LEN, weight, 0.0)
    return jnp.concatenate([weight * jnp.cos(phase), -weight * jnp.sin(phase)], axis=0)


def whiten(real_part, imag_part, seg_len):
    power = real_part * real_part + imag_part * imag_part
    bin_span = power.shape[1]
    padded = jnp.pad(power, ((0, 0), (2, 2)))
    smooth = (
        padded[:, 0:bin_span]
        + padded[:, 1 : bin_span + 1]
        + padded[:, 2 : bin_span + 2]
        + padded[:, 3 : bin_span + 3]
        + padded[:, 4 : bin_span + 4]
    ) / 5.0
    floor_level = water_level * (jnp.sum(power, axis=1, keepdims=True) / (seg_len + 1))
    inverse_norm = 1.0 / jnp.sqrt(jnp.maximum(smooth, floor_level) + epsilon)
    return (real_part * inverse_norm, imag_part * inverse_norm)


def whitened_spectra(traces):
    seg_len = traces.shape[1]
    blocks = (seg_len + block_width) // block_width
    real_parts = []
    imag_parts = []
    for block_index in range(blocks):
        product = jnp.dot(
            traces,
            forward_table(seg_len, block_index),
            precision=lax.Precision.HIGHEST,
            preferred_element_type=jnp.float32,
        )
        real_parts.append(product[:, :block_width])
        imag_parts.append(product[:, block_width:])
    real_part, imag_part = whiten(
        jnp.concatenate(real_parts, 1), jnp.concatenate(imag_parts, 1), seg_len
    )
    return jnp.stack([real_part, imag_part], axis=1)


def back_block(cross_re, cross_im, block_index, factor):
    joined = jnp.concatenate([cross_re, cross_im], axis=2)
    return jnp.einsum(
        "sck,kl->scl", joined, inverse_table(block_index, factor), precision=lax.Precision.HIGHEST
    )


def correlate(sources, channels, factor):
    blocks = sources.shape[2] // block_width
    total = jnp.zeros((sources.shape[0], channels.shape[0], 2 * MAXLAG + 1), jnp.float32)
    for block_index in range(blocks):
        first_bin = block_index * block_width
        src_re = sources[:, 0, first_bin : first_bin + block_width]
        src_im = sources[:, 1, first_bin : first_bin + block_width]
        chan_re = channels[:, 0, first_bin : first_bin + block_width]
        chan_im = channels[:, 1, first_bin : first_bin + block_width]
        cross_re = (
            src_re[:, None, :] * chan_re[None, :, :] + src_im[:, None, :] * chan_im[None, :, :]
        )
        cross_im = (
            src_re[:, None, :] * chan_im[None, :, :] - src_im[:, None, :] * chan_re[None, :, :]
        )
        total = total + back_block(cross_re, cross_im, block_index, factor)
    return total


def collect_sources(chan_spec, picked_index, inside):
    picked = jnp.where(inside[:, None, None], jnp.take(chan_spec, picked_index, axis=0), 0.0)
    return lax.psum(picked, "chan")


def body(strain, source_channels):
    channel_count = strain.shape[0]
    margin = TAPS - 3
    last_samples = strain[:, strain.shape[1] - margin :]
    before = from_behind(last_samples, "seg", 1)
    extended = jnp.concatenate([before, strain], axis=1)
    traces = decimate(extended, SEG_LEN)
    segments = lax.axis_size("seg")
    factor = 1.0 / math.sqrt(2.0 * SEG_LEN * segments)
    base = lax.axis_index("chan") * channel_count
    local = source_channels - base
    inside = (local >= 0) & (local < channel_count)
    picked_index = jnp.clip(local, 0, channel_count - 1)
    chan_spec = whitened_spectra(traces)
    collected = collect_sources(chan_spec, picked_index, inside)
    return lax.psum_scatter(
        correlate(collected, chan_spec, factor), "seg", scatter_dimension=0, tiled=True
    )


def solution(mesh):
    in_specs = (P("chan", "seg"), P())
    out_specs = P("seg", "chan", None)
    return jax.shard_map(body, mesh=mesh, in_specs=in_specs, out_specs=out_specs, check_vma=False)
```

profile of v0, /device:TPU:16, one launch (start us, length us, event | category | flops | bytes accessed | tf_op | source)
XLA Modules:
  0.0 421.2 jit_solution(7290643064510937001)
XLA Ops:
  6.5 0.0 all-reduce.4.cloned.1.call-start
  6.5 0.8 slice.131
  7.3 1.7 collective-permute-start
  9.3 0.7 compare_and_fusion
  9.9 1.4 cosine_select_fusion.4
  11.3 1.4 cosine_select_fusion
  12.6 1.4 cosine_select_fusion.1
  14.0 0.0 copy-start
  14.0 1.4 cosine_select_fusion.2
  15.4 1.4 cosine_select_fusion.3
  16.7 5.5 %cosine_multiply_fusion = (f32[128,501]{0,1:T(8,128)S(1)}, f32[128,501]{0,1:T(8,128)S(1)}, f32[128,501]{0,1:T(8,128)S(1)}, f32[128,501]{0,1:T(8,128)S(1)}, f32[1...) fusion(s32[128]{0:T(128)S(1)} %iota_add_fusion.1, ...), kind=kLoop, calls=%fused_computation.165 | loop fusion | flops 3527040 | bytes 2574292 | tf_op jit(solution)/shard_map/mul | solution.py:70
  22.2 0.7 fusion.176
  22.9 0.0 collective-permute-done
  22.9 0.0 copy-done
  22.9 0.1 fusion.153
  23.0 0.1 bitcast_dynamic-update-slice_fusion.2
  23.1 0.1 bitcast_dynamic-update-slice_fusion.1
  23.2 0.1 bitcast_dynamic-update-slice_fusion
  23.3 0.1 pad_maximum_fusion
  23.4 2.8 convolution_bitcast_fusion
  26.2 0.4 fusion.19
  26.7 0.4 fusion.35
  27.1 0.4 fusion.31
  27.5 0.4 fusion.27
  28.0 0.4 fusion.23
  28.4 0.1 fusion.211
  28.6 0.2 multiply_bitcast_fusion.1
  28.8 0.1 copy.4
  28.9 0.7 gather_fusion
  29.7 0.8 select_select_fusion
  30.5 0.0 all-reduce.4.cloned.1.call-update
  30.5 0.0 reduce-scatter.2.cloned.1.call-start
  30.6 306.1 %all-reduce.4.cloned.1.call-done = f32[32,2,640]{2,1,0:T(2,128)} async-done(((f32[32,2,640]{2,1,0:T(2,128)}), f32[32,2,640]{2,1,0:T(2,128)}) %all-reduce.4.cloned.1.call-update) | async-done | bytes 163856 | tf_op jit(solution)/shard_map/psum | solution.py:137
  336.7 1.1 fusion.212
  337.8 0.1 multiply_add_fusion.4
  337.9 1.9 fusion
  339.8 0.2 multiply_add_fusion
  340.0 1.9 fusion.12
  341.9 0.3 multiply_add_fusion.2
  342.2 1.9 fusion.8
  344.1 1.9 fusion.4
  346.0 3.7 add_add_fusion
  349.7 0.0 reduce-scatter.2.cloned.1.call-update
  349.7 64.7 %reduce-scatter.2.cloned.1.call-done = f32[2,32,501]{2,1,0:T(8,128)} async-done(((f32[32,32,501]{2,1,0:T(8,128)}), f32[2,32,501]{2,1,0:T(8,128)}) %reduce-scatter.2.cloned.1.call-update) | async-done | bytes 128272 | tf_op jit(solution)/shard_map/reduce_scatter | solution.py:155
  (29 shorter events, 0.2 us)
Async XLA Ops:
  6.5 330.2 %all-reduce.4.cloned.1.call-start = ((), (), s32[]{:S(2)}) async-start(), calls=%async_computation.1 | async-start | bytes 327680 | tf_op jit(solution)/shard_map/psum | solution.py:137
  7.3 15.6 %collective-permute-start = (f32[32,60]{1,0:T(8,128)S(1)}, f32[32,60]{1,0:T(8,128)S(1)}, u32[]{:S(2)}, u32[]{:S(2)}) collective-permute-start(f32[32,60]{1,0:T(8,128)S(1)} %slice.131), channel_id=1, source_target_pairs={{0,1},{1,2},{2,3},{3,4},{4,5},{5,6},{6,7},{7,8},{8,9},{9,10},{10,1... | collective-permute-start | bytes 23048 | tf_op jit(solution)/shard_map/ppermute | solution.py:19
  14.0 8.9 %copy-start = (f32[32,2500]{1,0:T(8,128)S(1)}, f32[32,2500]{1,0:T(8,128)}, u32[]{:S(2)}) copy-start(f32[32,2500]{1,0:T(8,128)} %param.2) | copy-start | bytes 960004
  30.5 383.8 %reduce-scatter.2.cloned.1.call-start = ((), (), s32[]{:S(2)}) async-start(), calls=%async_computation.2 | async-start | bytes 2228224 | tf_op jit(solution)/shard_map/reduce_scatter | solution.py:155
Sparse Core Ops, SparseCore 0:
  30.7 305.9 all-reduce.3
  349.8 64.5 reduce-scatter.1
where the time goes:
time: 421 us
  waiting for transfers between devices  371 us (88%)
  matrix products  16 us (4%)
  other arithmetic  15.7 us (4%)
  between operations  13.8 us (3%)
    psum x1, waiting for transfers between devices, collect_sources(): return lax.psum(picked, 'chan')  306 us
    reduce_scatter x1, waiting for transfers between devices, body(): lax.psum_scatter(correlate(collected, chan_spec, factor), 'seg', scatter_...  64.7 us
    dot_general x5, matrix products, back_block(): jnp.einsum('sck,kl->scl', joined, inverse_table(block_index, factor), pre...  11.2 us
  transfers between devices with their start and end apart: 3, of which 2 were waited for; matrix products, arithmetic and copies ran while one was open for 3% of the time, Pallas kernels for 0%

commit v1 on v0

--- a/solution.py
+++ b/solution.py
@@ -134,7 +134,8 @@
 
 def collect_sources(chan_spec, picked_index, inside):
     picked = jnp.where(inside[:, None, None], jnp.take(chan_spec, picked_index, axis=0), 0.0)
-    return lax.psum(picked, "chan")
+    tell_the_chunk = lambda x_local: jnp.sum(lax.all_gather(x_local, "chan"), axis=0)
+    return tell_the_chunk(picked)
 
 
 def body(strain, source_channels):

time: 421 us -> 230 us (0.55)
  waiting for transfers between devices: 371 us -> 177 us
    psum x1 -> x0, waiting for transfers between devices: 306 us -> none  [collect_sources(): return lax.psum(picked, 'chan')]
    all_gather x0 -> x1, waiting for transfers between devices: none -> 107 us  [collect_sources(): lax.all_gather(x_local, 'chan')]
    reduce_scatter x1, waiting for transfers between devices: 64.7 us -> 69.6 us  [body(): lax.psum_scatter(correlate(collected, chan_spec, factor), 'seg', scatter_...]
  transfers between devices with their start and end apart: 3 -> 3, of which waited for: 2 -> 2; matrix products, arithmetic and copies ran while one was open for 3% -> 6% of each run, Pallas kernels for 0% -> 0%
where the time goes in v1:
time: 230 us; the launch traced here: 229 us
  waiting for transfers between devices  177 us (77%)
  other arithmetic  17.8 us (8%)
  matrix products  16.3 us (7%)
  between operations  13.8 us (6%)
  local copies, waits for them, and re-layouts  2.74 us (1%)
    all_gather x1, waiting for transfers between devices, collect_sources(): lax.all_gather(x_local, 'chan')  107 us
    reduce_scatter x1, waiting for transfers between devices, body(): lax.psum_scatter(correlate(collected, chan_spec, factor), 'seg', scatter_...  69.6 us
    dot_general x5, matrix products, back_block(): jnp.einsum('sck,kl->scl', joined, inverse_table(block_index, factor), pre...  11.4 us
    select_n x5, other arithmetic, forward_table(): jnp.where(valid, jnp.cos(phase), 0.0)  6.77 us
    mul x1, other arithmetic, inverse_table(): weight * jnp.cos(phase)  5.32 us
  transfers between devices with their start and end apart: 3, of which 2 were waited for; matrix products, arithmetic and copies ran while one was open for 6% of the time, Pallas kernels for 0%

profile of v1, /device:TPU:16, one launch (start us, length us, event | category | flops | bytes accessed | tf_op | source)
XLA Modules:
  0.0 229.4 jit_solution(882237060225986424)
XLA Ops:
  6.5 0.0 copy-start
  6.5 0.0 all-gather.2.cloned.1.call-start
  6.5 0.9 slice.131
  7.4 1.7 collective-permute-start
  9.2 0.7 compare_and_fusion
  9.9 1.4 cosine_select_fusion.4
  11.3 1.4 cosine_select_fusion
  12.6 1.4 cosine_select_fusion.1
  14.0 1.4 cosine_select_fusion.2
  15.4 1.4 cosine_select_fusion.3
  16.7 0.8 fusion.177
  17.6 0.0 collective-permute-done
  17.6 0.0 copy-done
  17.6 0.1 fusion.154
  17.6 0.1 bitcast_dynamic-update-slice_fusion.2
  17.7 0.1 bitcast_dynamic-update-slice_fusion.1
  17.8 0.1 bitcast_dynamic-update-slice_fusion
  17.9 0.1 pad_maximum_fusion
  18.1 2.8 %convolution_bitcast_fusion = f32[5,4,8,128]{3,2,1,0:T(8,128)S(1)} fusion(f32[32,5,640]{2,0,1:T(8,128)S(1)} %fusion.156, f32[]{:T(128)} %fusion.177, s32[128]{0:T(128)S(1)} %iota_multiply_fusion), kind=kOutput, calls=%fused_computation.2 | convolution fusion | flops 161218560 | bytes 492036 | tf_op jit(solution)/shard_map/rbi,im->rbm/dot_general | solution.py:50
  20.9 0.4 fusion.19
  21.3 0.4 fusion.35
  21.8 0.4 fusion.31
  22.2 0.4 fusion.27
  22.6 0.4 fusion.23
  23.1 0.1 fusion.212
  23.2 0.2 multiply_bitcast_fusion.1
  23.5 0.1 copy.6
  23.6 0.7 gather_fusion
  24.3 0.2 fusion.123
  24.5 0.7 copy.7
  25.2 0.0 all-gather.2.cloned.1.call-update
  25.2 0.0 reduce-scatter.2.cloned.1.call-start
  25.3 5.3 %cosine_multiply_fusion = (f32[128,501]{0,1:T(8,128)S(1)}, f32[128,501]{0,1:T(8,128)S(1)}, f32[128,501]{0,1:T(8,128)S(1)}, f32[128,501]{0,1:T(8,128)S(1)}, f32[1...) fusion(s32[128]{0:T(128)S(1)} %iota_add_fusion.1, ...), kind=kLoop, calls=%fused_computation.165 | loop fusion | flops 3527040 | bytes 2574292 | tf_op jit(solution)/shard_map/mul | solution.py:70
  30.7 107.4 %all-gather.2.cloned.1.call-done = f32[32,32,2,640]{3,1,2,0:T(8,128)} async-done(((f32[1,32,2,640]{3,1,2,0:T(8,128)}), f32[32,32,2,640]{3,1,2,0:T(8,128)}) %all-gather.2.cloned.1.call-update) | async-done | bytes 5242896 | tf_op jit(solution)/shard_map/all_gather | solution.py:137
  138.1 2.8 %reduce_sum.29 = f32[32,2,640]{2,0,1:T(8,128)S(1)} reduce(f32[32,32,2,640]{3,1,2,0:T(8,128)} %all-gather.2.cloned.1.call-done, f32[]{:T(128)} %constant.121.clone.1), dimensions={0}, to_apply=%region_2.3 | reduce | flops 1269760 | bytes 5406724 | tf_op jit(solution)/shard_map/reduce_sum | solution.py:137
  140.9 0.2 multiply_add_fusion.4
  141.0 1.9 fusion
  142.9 0.3 multiply_add_fusion
  143.2 1.9 fusion.12
  145.1 0.2 multiply_add_fusion.2
  145.3 2.1 fusion.8
  147.4 1.9 fusion.4
  149.3 3.7 %add_add_fusion = f32[32,32,501]{2,1,0:T(8,128)} fusion(f32[32,32,501]{2,1,0:T(8,128)S(1)} %fusion.12, f32[32,32,501]{2,1,0:T(8,128)S(1)} %fusion.8, f32[32,32,501]{2,1,0:T(8,128)S(1)} %fusion, f32[32,32,501]{2,1,0:T(8,128)S(1)} %fusion.4, f32[32,32,128]{2,1,0:T(8,128)S(1)} %get-tuple-element.32, f32[32,32,128]{2,1,0:T(8,128)S(1)} %get-tuple-element.31, ...), kind=kOutput, calls=%fused_computation.1 | convolution fusion | flops 1578452224 | bytes 11822080 | tf_op jit(solution)/shard_map/sck,kl->scl/dot_general | solution.py:111
  153.0 0.0 reduce-scatter.2.cloned.1.call-update
  153.0 69.6 %reduce-scatter.2.cloned.1.call-done = f32[2,32,501]{2,1,0:T(8,128)} async-done(((f32[32,32,501]{2,1,0:T(8,128)}), f32[2,32,501]{2,1,0:T(8,128)}) %reduce-scatter.2.cloned.1.call-update) | async-done | bytes 128272 | tf_op jit(solution)/shard_map/reduce_scatter | solution.py:156
  (30 shorter events, 0.2 us)
Async XLA Ops:
  6.5 11.0 %copy-start = (f32[32,2500]{1,0:T(8,128)S(1)}, f32[32,2500]{1,0:T(8,128)}, u32[]{:S(2)}) copy-start(f32[32,2500]{1,0:T(8,128)} %param.2) | copy-start | bytes 960004
  6.5 131.5 %all-gather.2.cloned.1.call-start = ((), (), s32[]{:S(2)}) async-start(), calls=%async_computation.1 | async-start | bytes 5406720 | tf_op jit(solution)/shard_map/all_gather | solution.py:137
  7.4 10.2 %collective-permute-start = (f32[32,60]{1,0:T(8,128)S(1)}, f32[32,60]{1,0:T(8,128)S(1)}, u32[]{:S(2)}, u32[]{:S(2)}) collective-permute-start(f32[32,60]{1,0:T(8,128)S(1)} %slice.131), channel_id=1, source_target_pairs={{0,1},{1,2},{2,3},{3,4},{4,5},{5,6},{6,7},{7,8},{8,9},{9,10},{10,1... | collective-permute-start | bytes 23048 | tf_op jit(solution)/shard_map/ppermute | solution.py:19
  25.2 197.4 %reduce-scatter.2.cloned.1.call-start = ((), (), s32[]{:S(2)}) async-start(), calls=%async_computation.2 | async-start | bytes 2228224 | tf_op jit(solution)/shard_map/reduce_scatter | solution.py:156
Sparse Core Ops, SparseCore 0:
  25.3 112.6 all-gather.1
  153.1 69.3 reduce-scatter.1
